TPU v7x, 32 devices: a whole 2x2x4 slice. The times are simulated.
32 devices in a mesh: wide: 8 (over z, x), narrow: 4 (over y, core).
Axes of the slice: x: 2, y: 2, z: 4, core: 2. Of those that a mesh axis runs over, the one named last changes fastest.
Arguments:
- tokens: bfloat16 [64, 512, 768], P(('wide', 'narrow')), may hold values from -6 to 6
- doc_lengths: int32 [64], P(('wide', 'narrow')), may hold values from 30 to 512
- qkv_weight: bfloat16 [768, 2304], replicated, may hold values from -0.21875 to 0.21875
- query_bias: bfloat16 [768], replicated, may hold values from -3 to 3
- value_bias: bfloat16 [768], replicated, may hold values from -3 to 3
- out_weight: bfloat16 [768, 768], replicated, may hold values from -0.625 to 0.625
- out_bias: bfloat16 [768], replicated, may hold values from -1.75 to 1.75
- first_gain: bfloat16 [768], replicated, may hold values from 0.5 to 1.5
- first_shift: bfloat16 [768], replicated, may hold values from -1.75 to 1.75
- up_weight: bfloat16 [768, 3072], replicated, may hold values from -0.21875 to 0.21875
- up_bias: bfloat16 [3072], replicated, may hold values from -3 to 3
- down_weight: bfloat16 [3072, 768], replicated, may hold values from -0.15625 to 0.15625
- down_bias: bfloat16 [768], replicated, may hold values from -1.75 to 1.75
- second_gain: bfloat16 [768], replicated, may hold values from 0.5 to 1.5
- second_shift: bfloat16 [768], replicated, may hold values from -1.75 to 1.75
- dir_weight: bfloat16 [1536, 8], replicated, may hold values from -0.375 to 0.375
- dir_bias: bfloat16 [8], replicated, may hold values from -1 to 1
- segment_rows: int32 [64, 128], P(('wide', 'narrow')), may hold values from 0 to 511, as said below
- segment_slots: int32 [32, 256], P(('wide', 'narrow')), may hold values from 0 to 255, each once within a row
- pair_rows: int32 [32, 256, 2], P(('wide', 'narrow')), may hold values from 0 to 255
- pair_labels: int32 [32, 256], P(('wide', 'narrow')), may hold values from 0 to 7
- out_cotangent: bfloat16 [64, 512, 768], P(('wide', 'narrow')), may hold values from -6 to 6
Outputs:
- encoded: bfloat16 [64, 512, 768], P(('wide', 'narrow'))
- grad_tokens: bfloat16 [64, 512, 768], P(('wide', 'narrow'))
- grad_qkv_weight: float32 [768, 2304], P('narrow', 'wide')
- grad_query_bias: float32 [768], replicated
- grad_value_bias: float32 [768], replicated
- grad_out_weight: float32 [768, 768], P('narrow', 'wide')
- grad_out_bias: float32 [768], replicated
- grad_first_gain: float32 [768], replicated
- grad_first_shift: float32 [768], replicated
- grad_up_weight: float32 [768, 3072], P('narrow', 'wide')
- grad_up_bias: float32 [3072], replicated
- grad_down_weight: float32 [3072, 768], P('narrow', 'wide')
- grad_down_bias: float32 [768], replicated
- grad_second_gain: float32 [768], replicated
- grad_second_shift: float32 [768], replicated
- grad_dir_weight: float32 [1536, 8], replicated
- grad_dir_bias: float32 [8], replicated
Inputs may be any that keep to these rules, and one draw needn't show every extreme that they name: `segment_rows`: each value is below the token count of its document. `segment_slots`: each device's row holds every slot once.
All inputs are finite; a program needn't handle non-finite values.
Results may differ from a plain program's by a relative error of at most 0.02.
Values may be sent and summed in bfloat16 or wider, within the bound.
A program may use at most 192 MiB of HBM per device.

v0:
```python
import jax
import jax.numpy as jnp
from jax import lax
from jax.sharding import PartitionSpec as P

HEADS = 12
HEAD_DIM = 64
EXACT = lax.Precision.HIGHEST
MASKED = -1e30
EPSILON = 1e-05


def norm_forward(values, gain, shift):
    center = jnp.mean(values, -1, keepdims=True)
    centered = values - center
    inverse = lax.rsqrt(jnp.mean(centered * centered, -1, keepdims=True) + EPSILON)
    normed = centered * inverse
    return (normed * gain + shift, normed, inverse)


def norm_backward(grad, normed, inverse, gain):
    scaled = grad * gain
    first_mean = jnp.mean(scaled, -1, keepdims=True)
    second_mean = jnp.mean(scaled * normed, -1, keepdims=True)
    return (
        (scaled - first_mean - normed * second_mean) * inverse,
        jnp.sum(grad * normed, 0),
        jnp.sum(grad, 0),
    )


def normal_cdf(values):
    return 0.5 * (1.0 + lax.erf(values * 0.7071067811865476))


def on_device(
    tokens,
    doc_lengths,
    qkv_weight,
    query_bias,
    value_bias,
    out_weight,
    out_bias,
    first_gain,
    first_shift,
    up_weight,
    up_bias,
    down_weight,
    down_bias,
    second_gain,
    second_shift,
    dir_weight,
    dir_bias,
    segment_rows,
    segment_slots,
    pair_rows,
    pair_labels,
    out_cotangent,
):
    doc_count, length, model_width = tokens.shape
    score_scale = HEAD_DIM ** (-0.5)
    token_rows = tokens.reshape(doc_count * length, model_width)
    allowed = lax.broadcasted_iota(jnp.int32, (doc_count, length), 1) < doc_lengths[:, None]
    allowed_rows = allowed.reshape(-1, 1).astype(jnp.float32)
    bias_row = jnp.concatenate([query_bias, jnp.zeros_like(query_bias), value_bias]).astype(
        jnp.float32
    )
    qkv = (jnp.dot(token_rows, qkv_weight, preferred_element_type=jnp.float32) + bias_row).astype(
        jnp.bfloat16
    )

    def split_heads(doc_block, which):
        return doc_block[:, which * model_width : (which + 1) * model_width].reshape(
            length, HEADS, HEAD_DIM
        )

    def scores_of(queries, key_rows, doc_mask):
        scores = (
            jnp.einsum("qhd,khd->hqk", queries, key_rows, preferred_element_type=jnp.float32)
            * score_scale
        )
        return jnp.where(doc_mask[None, None, :], scores, MASKED)

    mixed_parts = []
    log_totals = []
    for doc_index in range(doc_count):
        doc_block = qkv[doc_index * length : (doc_index + 1) * length]
        queries = split_heads(doc_block, 0)
        key_rows = split_heads(doc_block, 1)
        value_rows = split_heads(doc_block, 2)
        scores = scores_of(queries, key_rows, allowed[doc_index])
        highest = jnp.max(scores, -1, keepdims=True)
        powers = jnp.exp(scores - highest)
        summed = jnp.sum(powers, -1, keepdims=True)
        attention = (powers / summed).astype(jnp.bfloat16)
        log_totals.append(highest + jnp.log(summed))
        mixed_parts.append(
            jnp.einsum(
                "hqk,khd->qhd", attention, value_rows, preferred_element_type=jnp.float32
            ).reshape(length, model_width)
        )
    mixed = jnp.concatenate(mixed_parts).astype(jnp.bfloat16)
    attended = jnp.dot(mixed, out_weight, preferred_element_type=jnp.float32) + out_bias.astype(
        jnp.float32
    )
    resid_one = token_rows.astype(jnp.float32) + attended
    hidden_one, normed_one, inverse_one = norm_forward(
        resid_one, first_gain.astype(jnp.float32), first_shift.astype(jnp.float32)
    )
    hidden_low = hidden_one.astype(jnp.bfloat16)
    upper_pre = jnp.dot(hidden_low, up_weight, preferred_element_type=jnp.float32) + up_bias.astype(
        jnp.float32
    )
    cumulative = normal_cdf(upper_pre)
    active = (upper_pre * cumulative).astype(jnp.bfloat16)
    lowered = jnp.dot(active, down_weight, preferred_element_type=jnp.float32) + down_bias.astype(
        jnp.float32
    )
    resid_two = hidden_one + lowered
    second_float = second_gain.astype(jnp.float32)
    normed_out, normed_two, inverse_two = norm_forward(
        resid_two, second_float, second_shift.astype(jnp.float32)
    )
    encoded_rows = (normed_out * allowed_rows).astype(jnp.bfloat16)
    doc_starts = lax.broadcasted_iota(jnp.int32, (doc_count, 1), 0) * length
    picked_rows = (segment_rows + doc_starts).reshape(-1)
    picked = encoded_rows[picked_rows]
    slots = segment_slots.reshape(-1)
    outgoing = jnp.zeros_like(picked).at[slots].set(picked)
    arrived = lax.all_to_all(outgoing, "wide", split_axis=0, concat_axis=0, tiled=True)
    pairs = pair_rows.reshape(-1, 2)
    labels = pair_labels.reshape(-1)
    first_rows = arrived[pairs[:, 0]]
    second_rows = arrived[pairs[:, 1]]
    logits = (
        jnp.dot(first_rows, dir_weight[:model_width], preferred_element_type=jnp.float32)
        + jnp.dot(second_rows, dir_weight[model_width:], preferred_element_type=jnp.float32)
        + dir_bias.astype(jnp.float32)
    )
    powers_head = jnp.exp(logits - jnp.max(logits, -1, keepdims=True))
    chance = powers_head / jnp.sum(powers_head, -1, keepdims=True)
    classes = lax.broadcasted_iota(jnp.int32, logits.shape, 1)
    delta = chance - (labels[:, None] == classes).astype(jnp.float32)
    first_float = first_rows.astype(jnp.float32)
    second_rows_float = second_rows.astype(jnp.float32)
    grad_dir_weight = jnp.concatenate(
        [
            jnp.dot(first_float.T, delta, precision=EXACT, preferred_element_type=jnp.float32),
            jnp.dot(
                second_rows_float.T, delta, precision=EXACT, preferred_element_type=jnp.float32
            ),
        ]
    )
    grad_dir_bias = jnp.sum(delta, 0)
    dir_float = dir_weight.astype(jnp.float32)
    grad_first = jnp.dot(
        delta, dir_float[:model_width].T, precision=EXACT, preferred_element_type=jnp.float32
    )
    grad_second = jnp.dot(
        delta, dir_float[model_width:].T, precision=EXACT, preferred_element_type=jnp.float32
    )
    grad_arrived = jnp.zeros((arrived.shape[0], model_width), jnp.float32)
    grad_arrived = grad_arrived.at[pairs[:, 0]].add(grad_first).at[pairs[:, 1]].add(grad_second)
    returned = lax.all_to_all(
        grad_arrived.astype(jnp.bfloat16), "wide", split_axis=0, concat_axis=0, tiled=True
    )
    grad_picked = returned[slots].astype(jnp.float32)
    grad_encoded = (
        out_cotangent.reshape(-1, model_width).astype(jnp.float32).at[picked_rows].add(grad_picked)
    )
    grad_encoded = grad_encoded * allowed_rows
    grad_two, grad_second_gain, grad_second_shift = norm_backward(
        grad_encoded, normed_two, inverse_two, second_float
    )
    grad_lowered = grad_two.astype(jnp.bfloat16)
    grad_down_weight = jnp.einsum(
        "rf,rd->fd", active, grad_lowered, preferred_element_type=jnp.float32
    )
    grad_down_bias = jnp.sum(grad_lowered.astype(jnp.float32), 0)
    grad_active = jnp.einsum(
        "rd,fd->rf", grad_lowered, down_weight, preferred_element_type=jnp.float32
    )
    density = jnp.exp(-0.5 * upper_pre * upper_pre) * 0.3989422804014327
    grad_upper = (grad_active * (cumulative + upper_pre * density)).astype(jnp.bfloat16)
    grad_up_weight = jnp.einsum(
        "rd,rf->df", hidden_low, grad_upper, preferred_element_type=jnp.float32
    )
    grad_up_bias = jnp.sum(grad_upper.astype(jnp.float32), 0)
    grad_hidden = grad_two + jnp.einsum(
        "rf,df->rd", grad_upper, up_weight, preferred_element_type=jnp.float32
    )
    grad_one, grad_first_gain, grad_first_shift = norm_backward(
        grad_hidden, normed_one, inverse_one, first_gain.astype(jnp.float32)
    )
    grad_attended = grad_one.astype(jnp.bfloat16)
    grad_out_weight = jnp.einsum(
        "rd,re->de", mixed, grad_attended, preferred_element_type=jnp.float32
    )
    grad_out_bias = jnp.sum(grad_attended.astype(jnp.float32), 0)
    grad_mixed = jnp.einsum(
        "re,de->rd", grad_attended, out_weight, preferred_element_type=jnp.float32
    ).astype(jnp.bfloat16)
    grad_parts = []
    for doc_index in range(doc_count):
        doc_block = qkv[doc_index * length : (doc_index + 1) * length]
        queries = split_heads(doc_block, 0)
        key_rows = split_heads(doc_block, 1)
        value_rows = split_heads(doc_block, 2)
        scores = scores_of(queries, key_rows, allowed[doc_index])
        attention = jnp.exp(scores - log_totals[doc_index])
        grad_doc = grad_mixed[doc_index * length : (doc_index + 1) * length].reshape(
            length, HEADS, HEAD_DIM
        )
        grad_chance = jnp.einsum(
            "qhd,khd->hqk", grad_doc, value_rows, preferred_element_type=jnp.float32
        )
        inner = jnp.sum(grad_chance * attention, -1, keepdims=True)
        grad_scores = (attention * (grad_chance - inner)).astype(jnp.bfloat16)
        grad_query = (
            jnp.einsum("hqk,khd->qhd", grad_scores, key_rows, preferred_element_type=jnp.float32)
            * score_scale
        )
        grad_key = (
            jnp.einsum("hqk,qhd->khd", grad_scores, queries, preferred_element_type=jnp.float32)
            * score_scale
        )
        grad_value = jnp.einsum(
            "hqk,qhd->khd",
            attention.astype(jnp.bfloat16),
            grad_doc,
            preferred_element_type=jnp.float32,
        )
        grad_parts.append(
            jnp.concatenate(
                [
                    grad_query.reshape(length, model_width),
                    grad_key.reshape(length, model_width),
                    grad_value.reshape(length, model_width),
                ],
                axis=1,
            )
        )
    grad_qkv = jnp.concatenate(grad_parts).astype(jnp.bfloat16)
    grad_qkv_float = grad_qkv.astype(jnp.float32)
    grad_query_bias = jnp.sum(grad_qkv_float[:, :model_width], 0)
    grad_value_bias = jnp.sum(grad_qkv_float[:, 2 * model_width :], 0)
    grad_qkv_weight = jnp.einsum(
        "rd,re->de", token_rows, grad_qkv, preferred_element_type=jnp.float32
    )
    grad_tokens = (
        jnp.einsum("re,de->rd", grad_qkv, qkv_weight, preferred_element_type=jnp.float32) + grad_one
    ).astype(jnp.bfloat16)
    matrices = (grad_qkv_weight, grad_out_weight, grad_up_weight, grad_down_weight)
    partial_sums = (
        lax.psum_scatter(
            matrices[0].astype(jnp.bfloat16), "wide", scatter_dimension=1, tiled=True
        ).astype(jnp.float32),
        lax.psum_scatter(
            matrices[1].astype(jnp.bfloat16), "wide", scatter_dimension=1, tiled=True
        ).astype(jnp.float32),
        lax.psum_scatter(
            matrices[2].astype(jnp.bfloat16), "wide", scatter_dimension=1, tiled=True
        ).astype(jnp.float32),
        lax.psum_scatter(
            matrices[3].astype(jnp.bfloat16), "wide", scatter_dimension=1, tiled=True
        ).astype(jnp.float32),
    )
    summed_mats = (
        lax.psum_scatter(
            partial_sums[0].astype(jnp.bfloat16), "narrow", scatter_dimension=0, tiled=True
        ).astype(jnp.float32),
        lax.psum_scatter(
            partial_sums[1].astype(jnp.bfloat16), "narrow", scatter_dimension=0, tiled=True
        ).astype(jnp.float32),
        lax.psum_scatter(
            partial_sums[2].astype(jnp.bfloat16), "narrow", scatter_dimension=0, tiled=True
        ).astype(jnp.float32),
        lax.psum_scatter(
            partial_sums[3].astype(jnp.bfloat16), "narrow", scatter_dimension=0, tiled=True
        ).astype(jnp.float32),
    )
    smalls = lax.psum(
        (
            grad_query_bias,
            grad_value_bias,
            grad_out_bias,
            grad_first_gain,
            grad_first_shift,
            grad_up_bias,
            grad_down_bias,
            grad_second_gain,
            grad_second_shift,
            grad_dir_weight,
            grad_dir_bias,
        ),
        ("wide", "narrow"),
    )
    return (
        encoded_rows.reshape(tokens.shape),
        grad_tokens.reshape(tokens.shape),
        summed_mats[0],
        smalls[0],
        smalls[1],
        summed_mats[1],
        smalls[2],
        smalls[3],
        smalls[4],
        summed_mats[2],
        smalls[5],
        summed_mats[3],
        smalls[6],
        smalls[7],
        smalls[8],
        smalls[9],
        smalls[10],
    )


def solution(mesh):
    placed = (
        P(("wide", "narrow"), None, None),
        P(("wide", "narrow")),
        P(),
        P(),
        P(),
        P(),
        P(),
        P(),
        P(),
        P(),
        P(),
        P(),
        P(),
        P(),
        P(),
        P(),
        P(),
        P(("wide", "narrow"), None),
        P(("wide", "narrow"), None),
        P(("wide", "narrow"), None, None),
        P(("wide", "narrow"), None),
        P(("wide", "narrow"), None, None),
    )
    return jax.shard_map(
        on_device,
        mesh=mesh,
        in_specs=placed,
        out_specs=(
            P(("wide", "narrow"), None, None),
            P(("wide", "narrow"), None, None),
            P("narrow", "wide"),
            P(),
            P(),
            P("narrow", "wide"),
            P(),
            P(),
            P(),
            P("narrow", "wide"),
            P(),
            P("narrow", "wide"),
            P(),
            P(),
            P(),
            P(),
            P(),
        ),
        check_vma=False,
    )
```

profile of v0, /device:TPU:0, one launch (start us, length us, event | category | flops | bytes accessed | tf_op | source)
XLA Modules:
  0.0 747.2 jit_solution(5606578285930874321)
XLA Ops:
  20.7 5.9 add_convert_fusion
  66.9 13.4 %multiply_convert_fusion.2 = (bf16[1024,3072]{1,0:T(8,128)(2,1)S(1)}, f32[1024,3072]{1,0:T(8,128)}) fusion(f32[3072]{0:T(1024)S(1)} %copy-done.46, bf16[768,3072]{1,0:T(8,128)(2,1)} %param.31, f32[1024,768]{1,0:T(8,128)S(1)} %get-tuple-element.114, f32[768]{0:T(1024)S(1)} %copy-done.50, f32[768]{0:T(1024)S(1)} %convert_element_type.164, ...), kind=kOutput, calls=%fused_computation.22 | convolution fusion | flops 4854644736 | bytes 26765312 | tf_op jit(solution)/shard_map/dot_general | solution.py:111
  94.2 7.7 %all-to-all-start = ((bf16[8,32,768]{2,1,0:T(8,128)(2,1)}), bf16[8,32,768]{2,1,0:T(8,128)(2,1)}, u32[]{:S(2)}, u32[]{:S(2)}) async-start(bf16[8,32,768]{2,1,0:T(8,128)(2,1)} %bitcast.144), calls=%async_computation | async-start | bytes 786432 | tf_op jit(solution)/shard_map/all_to_all | solution.py:130
  105.0 8.6 %all-to-all-done = bf16[8,32,768]{2,1,0:T(8,128)(2,1)} async-done(((bf16[8,32,768]{2,1,0:T(8,128)(2,1)}), bf16[8,32,768]{2,1,0:T(8,128)(2,1)}, u32[]{:S(2)}, u32[]{:S(2)}) %all-to-all-start) | async-done | bytes 393248 | tf_op jit(solution)/shard_map/all_to_all | solution.py:130
  154.0 8.2 %scatter_custom_fusion.3 = f32[1024,768]{1,0:T(8,128)} fusion(f32[1024,768]{1,0:T(8,128)} %bitcast_convert_fusion, s32[256]{0:T(256)} %bitcast.154, bf16[256,768]{1,0:T(8,128)(2,1)} %bitcast.24, s32[1024]{0:T(1024)} %pad_clamp_fusion), kind=kCustom, calls=%fused_computation.84 | custom fusion | flops 393216 | bytes 3543040 | tf_op jit(solution)/shard_map/scatter-add | solution.py:169
  169.4 13.5 %convert_reduce_fusion = (f32[3072]{0:T(1024)}, bf16[1024,3072]{1,0:T(8,128)(2,1)S(1)}) fusion(f32[1024,3072]{1,0:T(8,128)} %get-tuple-element.116, f32[3072]{0:T(1024)S(1)} %copy-done.47, bf16[3072,768]{1,0:T(8,128)(2,1)S(1)} %bitcast.165, f32[1024,768]{1,0:T(8,128)S(1)} %get-tuple-element.94), kind=kOutput, calls=%fused_computation.15 | convolution fusion | flops 4873516032 | bytes 26763264 | tf_op jit(solution)/shard_map/rd,fd->rf/dot_general | solution.py:180
  182.9 6.5 multiply_reduce_fusion.3
  199.3 10.6 %multiply_reduce_fusion.1 = (f32[12,512]{1,0:T(8,128)S(1)}, f32[12,512,512]{1,2,0:T(8,128)}) fusion(f32[12,512,512]{1,2,0:T(8,128)} %copy-done.1, f32[12,512]{1,0:T(8,128)S(1)} %copy-done.28, bf16[512,12,64]{0,2,1:T(8,128)(2,1)S(1)} %bitcast.114, bf16[512,12,64]{0,2,1:T(8,128)(2,1)S(1)} %bitcast.131), kind=kOutput, calls=%fused_computation.20 | convolution fusion | flops 412084224 | bytes 26787840 | tf_op jit(solution)/shard_map/qhd,khd->hqk/dot_general | solution.py:214
  212.2 10.8 %multiply_convert_fusion.1 = bf16[12,512,512]{1,2,0:T(8,128)(2,1)} fusion(f32[12,512,512]{1,2,0:T(8,128)} %get-tuple-element.125, f32[12,512,512]{1,2,0:T(8,128)S(1)} %bitcast.104, f32[12,512]{1,0:T(8,128)S(1)} %get-tuple-element.124, f32[12,512]{1,0:T(8,128)S(1)} %copy-done.28), kind=kLoop, calls=%fused_computation.19 | loop fusion | flops 12582912 | bytes 31506432 | tf_op jit(solution)/shard_map/convert_element_type | solution.py:218
  236.7 6.7 multiply_reduce_fusion
  243.4 10.7 %multiply_convert_fusion = bf16[12,512,512]{1,2,0:T(8,128)(2,1)S(1)} fusion(f32[12,512,512]{1,2,0:T(8,128)} %get-tuple-element.123, f32[12,512,512]{1,2,0:T(8,128)} %copy-done.2, f32[12,512]{1,0:T(8,128)} %get-tuple-element.122, f32[12,512]{1,0:T(8,128)} %log_add_fusion), kind=kLoop, calls=%fused_computation.16 | loop fusion | flops 12582912 | bytes 31506432 | tf_op jit(solution)/shard_map/convert_element_type | solution.py:218
  260.8 29.7 %fusion.18 = bf16[768,2304]{0,1:T(8,128)(2,1)} fusion(bf16[1024,768]{1,0:T(8,128)(2,1)S(1)} %bitcast.170, bf16[512,768]{0,1:T(8,128)(2,1)S(1)} %bitcast.134, bf16[512,768]{0,1:T(8,128)(2,1)S(1)} %bitcast.141, bf16[512,768]{0,1:T(8,128)(2,1)S(1)} %bitcast.125, bf16[512,768]{0,1:T(8,128)(2,1)S(1)} %bitcast.135, bf16[512,768]{0,1:T(8,128)(2,1)S(1)} %bitcast.140, ...), kind=kOutput, calls=%fused_computation.45 | convolution fusion | flops 3653959680 | bytes 9830400 | tf_op jit(solution)/shard_map/rd,re->de/dot_general | solution.py:247
  290.6 10.7 %convolution_convert_fusion.1 = bf16[768,3072]{1,0:T(8,128)(2,1)} fusion(bf16[1024,3072]{1,0:T(8,128)(2,1)} %copy-done.63, f32[1024,768]{1,0:T(8,128)} %copy-done.6, f32[768]{0:T(1024)} %convert_element_type.165, f32[768]{0:T(1024)S(1)} %copy-done.42, f32[1024]{0:T(1024)} %copy-done.43, f32[1024]{0:T(1024)S(1)} %copy-done.40), kind=kOutput, calls=%fused_computation.42 | convolution fusion | flops 4838129664 | bytes 14170112 | tf_op jit(solution)/shard_map/rd,rf->df/dot_general | solution.py:185
  301.3 6.7 copy.105
  308.0 10.1 %convolution_convert_fusion = bf16[3072,768]{0,1:T(8,128)(2,1)} fusion(bf16[1024,3072]{1,0:T(8,128)(2,1)} %copy-done.64, f32[1024,768]{1,0:T(8,128)} %copy-done.22), kind=kOutput, calls=%fused_computation.41 | convolution fusion | flops 4834983936 | bytes 14155776 | tf_op jit(solution)/shard_map/rf,rd->fd/dot_general | solution.py:176
  320.0 68.3 %reduce-scatter.15.cloned.1.call-done = bf16[768,288]{0,1:T(8,128)(2,1)} async-done(((bf16[768,2304]{0,1:T(8,128)(2,1)}), bf16[768,288]{0,1:T(8,128)(2,1)}) %reduce-scatter.15.cloned.1.call-update) | async-done | bytes 442384 | tf_op jit(solution)/shard_map/reduce_scatter | solution.py:255
  390.5 96.5 %reduce-scatter.29.cloned.1.call-done = bf16[384,768]{1,0:T(8,128)(2,1)} async-done(((bf16[3072,768]{1,0:T(8,128)(2,1)}), bf16[384,768]{1,0:T(8,128)(2,1)}) %reduce-scatter.29.cloned.1.call-update) | async-done | bytes 589840
  492.9 92.7 %reduce-scatter.21.cloned.1.call-done = bf16[3072,96]{0,1:T(8,128)(2,1)} async-done(((bf16[3072,768]{0,1:T(8,128)(2,1)}), bf16[3072,96]{0,1:T(8,128)(2,1)}) %reduce-scatter.21.cloned.1.call-update) | async-done | bytes 589840 | tf_op jit(solution)/shard_map/reduce_scatter | solution.py:264
  587.3 7.3 fusion.54
  598.5 8.4 %add_convert_fusion.1 = bf16[1024,768]{1,0:T(8,128)(2,1)} fusion(f32[1024,768]{1,0:T(8,128)} %copy-done.25, bf16[768,2304]{1,0:T(8,128)(2,1)S(1)} %copy-done, bf16[512,768]{0,1:T(8,128)(2,1)} %bitcast.133, bf16[512,768]{0,1:T(8,128)(2,1)} %bitcast.143, bf16[512,768]{0,1:T(8,128)(2,1)} %bitcast.127, bf16[512,768]{0,1:T(8,128)(2,1)} %bitcast.137, ...), kind=kOutput, calls=%fused_computation.52 | convolution fusion | flops 3653763072 | bytes 12976128 | tf_op jit(solution)/shard_map/re,de->rd/dot_general | solution.py:251
  611.2 21.5 %reduce-scatter.25.cloned.1.call-done = bf16[192,288]{1,0:T(8,128)(2,1)} async-done(((bf16[768,288]{1,0:T(8,128)(2,1)}), bf16[192,288]{1,0:T(8,128)(2,1)}) %reduce-scatter.25.cloned.1.call-update) | async-done | bytes 110608
  636.1 21.3 %reduce-scatter.19.cloned.1.call-done = bf16[192,384]{1,0:T(8,128)(2,1)} async-done(((bf16[768,384]{1,0:T(8,128)(2,1)}), bf16[192,384]{1,0:T(8,128)(2,1)}) %reduce-scatter.19.cloned.1.call-update) | async-done | bytes 147472 | tf_op jit(solution)/shard_map/reduce_scatter | solution.py:275
  659.0 23.2 %reduce-scatter.23.cloned.1.call-done = bf16[768,96]{0,1:T(8,128)(2,1)} async-done(((bf16[3072,96]{0,1:T(8,128)(2,1)}), bf16[768,96]{0,1:T(8,128)(2,1)}) %reduce-scatter.23.cloned.1.call-update) | async-done | bytes 147472 | tf_op jit(solution)/shard_map/reduce_scatter | solution.py:278
  683.8 41.7 %all-reduce.3.cloned.1.call-done = (f32[768]{0:T(1024)}, f32[768]{0:T(1024)}, f32[768]{0:T(1024)}, f32[768]{0:T(1024)}, f32[768]{0:T(1024)}, /*index=5*/f32[3072...) async-done(((f32[768]{0:T(1024)}, f32[768]{0:T(1024)}, f32[768]{0:T(1024)}, f32[768]{0:T(1024)}, f32[768]{0:T(1024)}, ...) | async-done | bytes 86064 | tf_op jit(solution)/shard_map/psum | solution.py:282
  (286 shorter events, 189.9 us)
Async XLA Ops:
  11.0 69.3 %copy-start.41 = (f32[768]{0:T(1024)}, f32[768]{0:T(1024)S(1)}, u32[]{:S(2)}) copy-start(f32[768]{0:T(1024)S(1)} %convert_element_type.164) | copy-start | bytes 9220
  18.1 68.2 %copy-start.35 = (f32[1,4,2,128]{3,1,2,0:T(4,128)}, f32[1,4,2,128]{3,1,2,0:T(4,128)S(1)}, u32[]{:S(2)}) copy-start(f32[1,4,2,128]{3,1,2,0:T(4,128)S(1)} %copy.107) | copy-start | bytes 12292
  28.8 13.9 %copy-start.55 = (pred[512]{0:T(512)(128)(4,1)S(1)}, pred[512]{0:T(512)(128)(4,1)}, u32[]{:S(2)}) copy-start(pred[512]{0:T(512)(128)(4,1)} %get-tuple-element.78) | copy-start | bytes 1540
  66.2 14.0 %copy-start.6 = (f32[1024,768]{1,0:T(8,128)}, f32[1024,768]{1,0:T(8,128)S(1)}, u32[]{:S(2)}) copy-start(f32[1024,768]{1,0:T(8,128)S(1)} %get-tuple-element.114) | copy-start | bytes 9437188
  66.3 14.0 %copy-start.39 = (f32[1024]{0:T(1024)}, f32[1024]{0:T(1024)S(1)}, u32[]{:S(2)}) copy-start(f32[1024]{0:T(1024)S(1)} %broadcast_multiply_fusion.5) | copy-start | bytes 12292
  66.3 14.0 %slice-start.9 = ((s8[4718592]{0:T(1024)(128)(4,1)}), s8[4194304]{0:T(1024)(128)(4,1)S(1)}, s32[]{:S(2)}) async-start(s8[4718592]{0:T(1024)(128)(4,1)} %bitcast.162), calls=%async_computation.28 | async-start | bytes 8388608
  86.4 30.6 %copy-start.37 = (f32[1024]{0:T(1024)}, f32[1024]{0:T(1024)S(1)}, u32[]{:S(2)}) copy-start(f32[1024]{0:T(1024)S(1)} %add_rsqrt_fusion) | copy-start | bytes 12292
  94.2 19.4 %all-to-all-start = ((bf16[8,32,768]{2,1,0:T(8,128)(2,1)}), bf16[8,32,768]{2,1,0:T(8,128)(2,1)}, u32[]{:S(2)}, u32[]{:S(2)}) async-start(bf16[8,32,768]{2,1,0:T(8,128)(2,1)} %bitcast.144), calls=%async_computation | async-start | bytes 786432 | tf_op jit(solution)/shard_map/all_to_all | solution.py:130
  138.7 15.3 %all-to-all-start.1 = ((bf16[8,32,768]{2,1,0:T(8,128)(2,1)}), bf16[8,32,768]{2,1,0:T(8,128)(2,1)}, u32[]{:S(2)}, u32[]{:S(2)}) async-start(bf16[8,32,768]{2,1,0:T(8,128)(2,1)} %bitcast.145), calls=%async_computation.1 | async-start | bytes 786432 | tf_op jit(solution)/shard_map/all_to_all | solution.py:164
  142.8 175.4 %reduce-scatter.17.cloned.1.call-start = ((), (), s32[]{:S(2)}) async-start(), calls=%async_computation.11 | async-start | bytes 1327104 | tf_op jit(solution)/shard_map/reduce_scatter | solution.py:258
  167.4 15.4 %slice-start.13 = ((s8[4718592]{0:T(1024)(128)(4,1)}), s8[4194304]{0:T(1024)(128)(4,1)S(1)}, s32[]{:S(2)}) async-start(s8[4718592]{0:T(1024)(128)(4,1)} %bitcast.166), calls=%async_computation.32 | async-start | bytes 8388608
  169.3 13.5 %copy-start.22 = (f32[1024,768]{1,0:T(8,128)}, f32[1024,768]{1,0:T(8,128)S(1)}, u32[]{:S(2)}) copy-start(f32[1024,768]{1,0:T(8,128)S(1)} %get-tuple-element.94) | copy-start | bytes 9437188
  212.2 21.5 %slice-start.6 = ((s8[12582912]{0:T(1024)(128)(4,1)}), s8[4194304]{0:T(1024)(128)(4,1)S(1)}, s32[]{:S(2)}) async-start(s8[12582912]{0:T(1024)(128)(4,1)} %bitcast.107), calls=%async_computation.25 | async-start | bytes 8388608
  212.2 21.5 %slice-start.7 = ((s8[12582912]{0:T(1024)(128)(4,1)}), s8[4194304]{0:T(1024)(128)(4,1)S(1)}, s32[]{:S(2)}) async-start(s8[12582912]{0:T(1024)(128)(4,1)} %bitcast.107), calls=%async_computation.26 | async-start | bytes 8388608
  243.4 145.0 %reduce-scatter.15.cloned.1.call-start = ((), (), s32[]{:S(2)}) async-start(), calls=%async_computation.10 | async-start | bytes 3981312 | tf_op jit(solution)/shard_map/reduce_scatter | solution.py:255
  243.4 14.0 %slice-start.3 = ((s8[12582912]{0:T(1024)(128)(4,1)}), s8[4194304]{0:T(1024)(128)(4,1)S(1)}, s32[]{:S(2)}) async-start(s8[12582912]{0:T(1024)(128)(4,1)} %bitcast.105), calls=%async_computation.22 | async-start | bytes 8388608
  243.4 14.0 %slice-start.4 = ((s8[12582912]{0:T(1024)(128)(4,1)}), s8[4194304]{0:T(1024)(128)(4,1)S(1)}, s32[]{:S(2)}) async-start(s8[12582912]{0:T(1024)(128)(4,1)} %bitcast.105), calls=%async_computation.23 | async-start | bytes 8388608
  290.6 196.4 %reduce-scatter.29.cloned.1.call-start = ((), (), s32[]{:S(2)}) async-start(), calls=%async_computation.17 | async-start | bytes 5308416
  308.0 277.7 %reduce-scatter.21.cloned.1.call-start = ((), (), s32[]{:S(2)}) async-start(), calls=%async_computation.13 | async-start | bytes 5308416 | tf_op jit(solution)/shard_map/reduce_scatter | solution.py:264
  318.1 290.0 %reduce-scatter.27.cloned.1.call-start = ((), (), s32[]{:S(2)}) async-start(), calls=%async_computation.16 | async-start | bytes 245760
  320.0 312.7 %reduce-scatter.25.cloned.1.call-start = ((), (), s32[]{:S(2)}) async-start(), calls=%async_computation.15 | async-start | bytes 737280
  390.4 267.0 %reduce-scatter.19.cloned.1.call-start = ((), (), s32[]{:S(2)}) async-start(), calls=%async_computation.12 | async-start | bytes 737280 | tf_op jit(solution)/shard_map/reduce_scatter | solution.py:275
  489.1 193.1 %reduce-scatter.23.cloned.1.call-start = ((), (), s32[]{:S(2)}) async-start(), calls=%async_computation.14 | async-start | bytes 737280 | tf_op jit(solution)/shard_map/reduce_scatter | solution.py:278
  585.7 139.9 %all-reduce.3.cloned.1.call-start = ((), (), s32[]{:S(2)}) async-start(), calls=%async_computation.18 | async-start | bytes 189440 | tf_op jit(solution)/shard_map/psum | solution.py:282
  (67 other events, 387.4 us)
Sparse Core Ops, SparseCore 0:
  243.5 63.0 reduce-scatter.16
  310.2 78.0 reduce-scatter.14
  392.0 94.9 reduce-scatter.28
  490.5 95.1 reduce-scatter.20
  588.5 19.5 reduce-scatter.26
  610.5 22.1 reduce-scatter.24
  635.3 22.0 reduce-scatter.18
  660.1 22.0 reduce-scatter.22
Sparse Core Ops, SparseCore 1:
  598.5 126.9 all-reduce.2
where the time goes:
time: 756 us; the launch traced here: 747 us
  waiting for transfers between devices  379 us (50%)
  matrix products  170 us (22%)
  other arithmetic  94.5 us (12%)
  local copies, waits for them, and re-layouts  74.2 us (10%)
  between operations  16.8 us (2%)
  starting transfers between devices  12.4 us (2%)
    unnamed x12, waiting for transfers between devices  119 us
    reduce_scatter x1, waiting for transfers between devices, on_device(): lax.psum_scatter(matrices[3].astype(jnp.bfloat16), 'wide', scatter_dimens...  92.7 us
    reduce_scatter x1, waiting for transfers between devices, on_device(): lax.psum_scatter(matrices[0].astype(jnp.bfloat16), 'wide', scatter_dimens...  68.3 us
    unnamed x180, local copies, waits for them, and re-layouts  46 us
    psum x1, waiting for transfers between devices, on_device(): lax.psum((grad_query_bias, grad_value_bias, grad_out_bias, grad_first_gai...  41.7 us
    dot_general x1, matrix products, on_device(): jnp.einsum('rd,re->de', token_rows, grad_qkv, preferred_element_type=jnp....  29.7 us
    reduce_scatter x1, waiting for transfers between devices, on_device(): lax.psum_scatter(partial_sums[3].astype(jnp.bfloat16), 'narrow', scatter_...  23.2 us
    convert_element_type x2, other arithmetic, on_device(): grad_scores = (attention * (grad_chance - inner)).astype(jnp.bfloat16)  21.5 us
  transfers between devices with their start and end apart: 11, of which 10 were waited for; matrix products, arithmetic and copies ran while one was open for 16% of the time, Pallas kernels for 0%

commit v1 on v0

--- a/solution.py
+++ b/solution.py
@@ -8,6 +8,17 @@
 EXACT = lax.Precision.HIGHEST
 MASKED = -1e30
 EPSILON = 1e-05
+
+
+def cut_along(value, dim, size):
+    before, after = (value.shape[:dim], value.shape[dim + 1 :])
+    return jnp.moveaxis(value.reshape(*before, size, -1, *after), dim, 0)
+
+
+def joined_along(pieces, dim):
+    pieces = jnp.moveaxis(pieces, 0, dim)
+    lengths = pieces.shape
+    return pieces.reshape(*lengths[:dim], lengths[dim] * lengths[dim + 1], *lengths[dim + 2 :])
 
 
 def norm_forward(values, gain, shift):
@@ -127,7 +138,14 @@
     picked = encoded_rows[picked_rows]
     slots = segment_slots.reshape(-1)
     outgoing = jnp.zeros_like(picked).at[slots].set(picked)
-    arrived = lax.all_to_all(outgoing, "wide", split_axis=0, concat_axis=0, tiled=True)
+    size, place = (lax.axis_size("wide"), lax.axis_index("wide"))
+    blocks = cut_along(outgoing, 0, size)
+    outs = [blocks[place]]
+    for lap in range(1, size):
+        sent = blocks[place ^ lap]
+        outs.append(lax.ppermute(sent, "wide", [(i, i ^ lap) for i in range(size)]))
+    blocks = jnp.stack(outs)[place ^ jnp.arange(size)]
+    arrived = joined_along(blocks, 0)
     pairs = pair_rows.reshape(-1, 2)
     labels = pair_labels.reshape(-1)
     first_rows = arrived[pairs[:, 0]]

time: 756 us -> 769 us (1.017)
  local copies, waits for them, and re-layouts: 74.2 us -> 82.6 us
    ppermute x0 -> x7, starting transfers between devices: none -> 12.9 us  [on_device(): outs.append(lax.ppermute(sent, 'wide', [(i, i ^ lap) for i in range(size)]))]
    all_to_all x1 -> x0, waiting for transfers between devices: 8.62 us -> none  [on_device(): lax.all_to_all(outgoing, 'wide', split_axis=0, concat_axis=0, tiled=True)]
    all_to_all x1 -> x0, starting transfers between devices: 7.7 us -> none  [on_device(): lax.all_to_all(outgoing, 'wide', split_axis=0, concat_axis=0, tiled=True)]
  transfers between devices with their start and end apart: 11 -> 17, of which waited for: 10 -> 11; matrix products, arithmetic and copies ran while one was open for 16% -> 17% of each run, Pallas kernels for 0% -> 0%
where the time goes in v1:
time: 769 us; the launch traced here: 760 us
  waiting for transfers between devices  374 us (49%)
  matrix products  170 us (22%)
  other arithmetic  97.7 us (13%)
  local copies, waits for them, and re-layouts  82.6 us (11%)
  starting transfers between devices  18.5 us (2%)
  between operations  16.9 us (2%)
    unnamed x12, waiting for transfers between devices  119 us
    reduce_scatter x1, waiting for transfers between devices, on_device(): lax.psum_scatter(matrices[3].astype(jnp.bfloat16), 'wide', scatter_dimens...  92.5 us
    reduce_scatter x1, waiting for transfers between devices, on_device(): lax.psum_scatter(matrices[0].astype(jnp.bfloat16), 'wide', scatter_dimens...  69.1 us
    unnamed x180, local copies, waits for them, and re-layouts  49.7 us
    psum x1, waiting for transfers between devices, on_device(): lax.psum((grad_query_bias, grad_value_bias, grad_out_bias, grad_first_gai...  41.6 us
    dot_general x1, matrix products, on_device(): jnp.einsum('rd,re->de', token_rows, grad_qkv, preferred_element_type=jnp....  29.7 us
    reduce_scatter x1, waiting for transfers between devices, on_device(): lax.psum_scatter(partial_sums[3].astype(jnp.bfloat16), 'narrow', scatter_...  23.2 us
    convert_element_type x2, other arithmetic, on_device(): grad_scores = (attention * (grad_chance - inner)).astype(jnp.bfloat16)  21.5 us
  transfers between devices with their start and end apart: 17, of which 11 were waited for; matrix products, arithmetic and copies ran while one was open for 17% of the time, Pallas kernels for 0%

profile of v1, /device:TPU:0, one launch (start us, length us, event | category | flops | bytes accessed | tf_op | source)
XLA Modules:
  0.0 760.3 jit_solution(12080092621451816105)
XLA Ops:
  19.5 5.9 add_convert_fusion
  65.7 13.4 %multiply_convert_fusion.2 = (bf16[1024,3072]{1,0:T(8,128)(2,1)S(1)}, f32[1024,3072]{1,0:T(8,128)}) fusion(f32[3072]{0:T(1024)S(1)} %copy-done.45, bf16[768,3072]{1,0:T(8,128)(2,1)} %param.31, f32[1024,768]{1,0:T(8,128)S(1)} %get-tuple-element.122, f32[768]{0:T(1024)S(1)} %copy-done.48, f32[768]{0:T(1024)S(1)} %convert_element_type.164, ...), kind=kOutput, calls=%fused_computation.23 | convolution fusion | flops 4854644736 | bytes 26765312 | tf_op jit(solution)/shard_map/dot_general | solution.py:122
  98.0 6.0 collective-permute-start.6
  166.9 8.2 %scatter_custom_fusion.3 = f32[1024,768]{1,0:T(8,128)} fusion(f32[1024,768]{1,0:T(8,128)} %bitcast_convert_fusion, s32[256]{0:T(256)} %bitcast.186, bf16[256,768]{1,0:T(8,128)(2,1)} %bitcast.39, s32[1024]{0:T(1024)} %pad_clamp_fusion), kind=kCustom, calls=%fused_computation.85 | custom fusion | flops 393216 | bytes 3543040 | tf_op jit(solution)/shard_map/scatter-add | solution.py:187
  182.2 13.4 %convert_reduce_fusion = (f32[3072]{0:T(1024)}, bf16[1024,3072]{1,0:T(8,128)(2,1)S(1)}) fusion(f32[1024,3072]{1,0:T(8,128)} %get-tuple-element.124, f32[3072]{0:T(1024)S(1)} %copy-done.46, bf16[3072,768]{1,0:T(8,128)(2,1)S(1)} %bitcast.197, f32[1024,768]{1,0:T(8,128)S(1)} %get-tuple-element.94), kind=kOutput, calls=%fused_computation.16 | convolution fusion | flops 4873516032 | bytes 26763264 | tf_op jit(solution)/shard_map/rd,fd->rf/dot_general | solution.py:198
  195.7 6.5 multiply_reduce_fusion.3
  212.1 10.6 %multiply_reduce_fusion.1 = (f32[12,512]{1,0:T(8,128)S(1)}, f32[12,512,512]{1,2,0:T(8,128)}) fusion(f32[12,512,512]{1,2,0:T(8,128)} %copy-done.1, f32[12,512]{1,0:T(8,128)S(1)} %copy-done.28, bf16[512,12,64]{0,2,1:T(8,128)(2,1)S(1)} %bitcast.146, bf16[512,12,64]{0,2,1:T(8,128)(2,1)S(1)} %bitcast.163), kind=kOutput, calls=%fused_computation.21 | convolution fusion | flops 412084224 | bytes 26787840 | tf_op jit(solution)/shard_map/qhd,khd->hqk/dot_general | solution.py:232
  225.0 10.8 %multiply_convert_fusion.1 = bf16[12,512,512]{1,2,0:T(8,128)(2,1)} fusion(f32[12,512,512]{1,2,0:T(8,128)} %get-tuple-element.133, f32[12,512,512]{1,2,0:T(8,128)S(1)} %bitcast.134, f32[12,512]{1,0:T(8,128)S(1)} %get-tuple-element.132, f32[12,512]{1,0:T(8,128)S(1)} %copy-done.28), kind=kLoop, calls=%fused_computation.20 | loop fusion | flops 12582912 | bytes 31506432 | tf_op jit(solution)/shard_map/convert_element_type | solution.py:236
  235.8 5.8 multiply_convert_fusion.6
  249.5 6.7 multiply_reduce_fusion
  256.2 10.7 %multiply_convert_fusion = bf16[12,512,512]{1,2,0:T(8,128)(2,1)S(1)} fusion(f32[12,512,512]{1,2,0:T(8,128)} %get-tuple-element.131, f32[12,512,512]{1,2,0:T(8,128)} %copy-done.2, f32[12,512]{1,0:T(8,128)} %get-tuple-element.130, f32[12,512]{1,0:T(8,128)} %log_add_fusion), kind=kLoop, calls=%fused_computation.17 | loop fusion | flops 12582912 | bytes 31506432 | tf_op jit(solution)/shard_map/convert_element_type | solution.py:236
  273.6 29.7 %fusion.18 = bf16[768,2304]{0,1:T(8,128)(2,1)} fusion(bf16[1024,768]{1,0:T(8,128)(2,1)S(1)} %bitcast.202, bf16[512,768]{0,1:T(8,128)(2,1)S(1)} %bitcast.166, bf16[512,768]{0,1:T(8,128)(2,1)S(1)} %bitcast.173, bf16[512,768]{0,1:T(8,128)(2,1)S(1)} %bitcast.157, bf16[512,768]{0,1:T(8,128)(2,1)S(1)} %bitcast.167, bf16[512,768]{0,1:T(8,128)(2,1)S(1)} %bitcast.172, ...), kind=kOutput, calls=%fused_computation.46 | convolution fusion | flops 3653959680 | bytes 9830400 | tf_op jit(solution)/shard_map/rd,re->de/dot_general | solution.py:265
  303.4 10.6 %convolution_convert_fusion.1 = bf16[768,3072]{1,0:T(8,128)(2,1)} fusion(bf16[1024,3072]{1,0:T(8,128)(2,1)} %copy-done.60, f32[1024,768]{1,0:T(8,128)} %copy-done.6, f32[768]{0:T(1024)} %convert_element_type.165, f32[768]{0:T(1024)S(1)} %copy-done.42, f32[1024]{0:T(1024)} %copy-done.43, f32[1024]{0:T(1024)S(1)} %copy-done.40), kind=kOutput, calls=%fused_computation.43 | convolution fusion | flops 4838129664 | bytes 14170112 | tf_op jit(solution)/shard_map/rd,rf->df/dot_general | solution.py:203
  314.0 6.7 copy.105
  320.7 10.1 %convolution_convert_fusion = bf16[3072,768]{0,1:T(8,128)(2,1)} fusion(bf16[1024,3072]{1,0:T(8,128)(2,1)} %copy-done.61, f32[1024,768]{1,0:T(8,128)} %copy-done.22), kind=kOutput, calls=%fused_computation.42 | convolution fusion | flops 4834983936 | bytes 14155776 | tf_op jit(solution)/shard_map/rf,rd->fd/dot_general | solution.py:194
  332.7 69.1 %reduce-scatter.15.cloned.1.call-done = bf16[768,288]{0,1:T(8,128)(2,1)} async-done(((bf16[768,2304]{0,1:T(8,128)(2,1)}), bf16[768,288]{0,1:T(8,128)(2,1)}) %reduce-scatter.15.cloned.1.call-update) | async-done | bytes 442384 | tf_op jit(solution)/shard_map/reduce_scatter | solution.py:273
  404.0 96.3 %reduce-scatter.29.cloned.1.call-done = bf16[384,768]{1,0:T(8,128)(2,1)} async-done(((bf16[3072,768]{1,0:T(8,128)(2,1)}), bf16[384,768]{1,0:T(8,128)(2,1)}) %reduce-scatter.29.cloned.1.call-update) | async-done | bytes 589840
  506.3 92.5 %reduce-scatter.21.cloned.1.call-done = bf16[3072,96]{0,1:T(8,128)(2,1)} async-done(((bf16[3072,768]{0,1:T(8,128)(2,1)}), bf16[3072,96]{0,1:T(8,128)(2,1)}) %reduce-scatter.21.cloned.1.call-update) | async-done | bytes 589840 | tf_op jit(solution)/shard_map/reduce_scatter | solution.py:282
  600.5 7.3 fusion.55
  611.6 8.4 %add_convert_fusion.1 = bf16[1024,768]{1,0:T(8,128)(2,1)} fusion(f32[1024,768]{1,0:T(8,128)} %copy-done.25, bf16[768,2304]{1,0:T(8,128)(2,1)S(1)} %copy-done, bf16[512,768]{0,1:T(8,128)(2,1)} %bitcast.165, bf16[512,768]{0,1:T(8,128)(2,1)} %bitcast.175, bf16[512,768]{0,1:T(8,128)(2,1)} %bitcast.159, bf16[512,768]{0,1:T(8,128)(2,1)} %bitcast.169, ...), kind=kOutput, calls=%fused_computation.53 | convolution fusion | flops 3653763072 | bytes 12976128 | tf_op jit(solution)/shard_map/re,de->rd/dot_general | solution.py:269
  624.4 21.5 %reduce-scatter.25.cloned.1.call-done = bf16[192,288]{1,0:T(8,128)(2,1)} async-done(((bf16[768,288]{1,0:T(8,128)(2,1)}), bf16[192,288]{1,0:T(8,128)(2,1)}) %reduce-scatter.25.cloned.1.call-update) | async-done | bytes 110608
  649.2 21.3 %reduce-scatter.19.cloned.1.call-done = bf16[192,384]{1,0:T(8,128)(2,1)} async-done(((bf16[768,384]{1,0:T(8,128)(2,1)}), bf16[192,384]{1,0:T(8,128)(2,1)}) %reduce-scatter.19.cloned.1.call-update) | async-done | bytes 147472 | tf_op jit(solution)/shard_map/reduce_scatter | solution.py:293
  672.2 23.2 %reduce-scatter.23.cloned.1.call-done = bf16[768,96]{0,1:T(8,128)(2,1)} async-done(((bf16[3072,96]{0,1:T(8,128)(2,1)}), bf16[768,96]{0,1:T(8,128)(2,1)}) %reduce-scatter.23.cloned.1.call-update) | async-done | bytes 147472 | tf_op jit(solution)/shard_map/reduce_scatter | solution.py:296
  697.0 41.6 %all-reduce.3.cloned.1.call-done = (f32[768]{0:T(1024)}, f32[768]{0:T(1024)}, f32[768]{0:T(1024)}, f32[768]{0:T(1024)}, f32[768]{0:T(1024)}, /*index=5*/f32[3072...) async-done(((f32[768]{0:T(1024)}, f32[768]{0:T(1024)}, f32[768]{0:T(1024)}, f32[768]{0:T(1024)}, f32[768]{0:T(1024)}, ...) | async-done | bytes 86064 | tf_op jit(solution)/shard_map/psum | solution.py:300
  (303 shorter events, 207.2 us)
Async XLA Ops:
  9.8 69.3 %copy-start.41 = (f32[768]{0:T(1024)}, f32[768]{0:T(1024)S(1)}, u32[]{:S(2)}) copy-start(f32[768]{0:T(1024)S(1)} %convert_element_type.164) | copy-start | bytes 9220
  16.9 71.4 %copy-start.35 = (f32[1,4,2,128]{3,1,2,0:T(4,128)}, f32[1,4,2,128]{3,1,2,0:T(4,128)S(1)}, u32[]{:S(2)}) copy-start(f32[1,4,2,128]{3,1,2,0:T(4,128)S(1)} %copy.107) | copy-start | bytes 12292
  65.0 14.0 %copy-start.6 = (f32[1024,768]{1,0:T(8,128)}, f32[1024,768]{1,0:T(8,128)S(1)}, u32[]{:S(2)}) copy-start(f32[1024,768]{1,0:T(8,128)S(1)} %get-tuple-element.122) | copy-start | bytes 9437188
  86.9 43.6 %copy-start.37 = (f32[1024]{0:T(1024)}, f32[1024]{0:T(1024)S(1)}, u32[]{:S(2)}) copy-start(f32[1024]{0:T(1024)S(1)} %add_rsqrt_fusion) | copy-start | bytes 12292
  98.0 26.0 %collective-permute-start.6 = (bf16[32,768]{1,0:T(8,128)(2,1)S(1)}, bf16[32,768]{1,0:T(8,128)(2,1)S(1)}, u32[]{:S(2)}, u32[]{:S(2)}) collective-permute-start(bf16[32,768]{1,0:T(8,128)(2,1)S(1)} %get-tuple-element.105), channel_id=1, source_target_pairs={{0,28},{4,24},{8,20},{12,16},{16,12},{20,8},{24,4},{28,0},{1,29},{... | collective-permute-start | bytes 147464 | tf_op jit(solution)/shard_map/ppermute | solution.py:146
  104.0 19.4 %collective-permute-start.5 = (bf16[32,768]{1,0:T(8,128)(2,1)S(1)}, bf16[32,768]{1,0:T(8,128)(2,1)S(1)}, u32[]{:S(2)}, u32[]{:S(2)}) collective-permute-start(bf16[32,768]{1,0:T(8,128)(2,1)S(1)} %get-tuple-element.106), channel_id=1, source_target_pairs={{0,24},{4,28},{8,16},{12,20},{16,8},{20,12},{24,0},{28,4},{1,25},{... | collective-permute-start | bytes 147464 | tf_op jit(solution)/shard_map/ppermute | solution.py:146
  104.2 18.6 %collective-permute-start.4 = (bf16[32,768]{1,0:T(8,128)(2,1)S(1)}, bf16[32,768]{1,0:T(8,128)(2,1)S(1)}, u32[]{:S(2)}, u32[]{:S(2)}) collective-permute-start(bf16[32,768]{1,0:T(8,128)(2,1)S(1)} %get-tuple-element.107), channel_id=1, source_target_pairs={{0,20},{4,16},{8,28},{12,24},{16,4},{20,0},{24,12},{28,8},{1,21},{... | collective-permute-start | bytes 147464 | tf_op jit(solution)/shard_map/ppermute | solution.py:146
  105.0 17.2 %collective-permute-start.3 = (bf16[32,768]{1,0:T(8,128)(2,1)S(1)}, bf16[32,768]{1,0:T(8,128)(2,1)S(1)}, u32[]{:S(2)}, u32[]{:S(2)}) collective-permute-start(bf16[32,768]{1,0:T(8,128)(2,1)S(1)} %get-tuple-element.108), channel_id=1, source_target_pairs={{0,16},{4,20},{8,24},{12,28},{16,0},{20,4},{24,8},{28,12},{1,17},{... | collective-permute-start | bytes 147464 | tf_op jit(solution)/shard_map/ppermute | solution.py:146
  106.9 5.4 collective-permute-start
  112.4 4.2 collective-permute-start.1
  116.6 5.0 collective-permute-start.2
  152.6 14.3 %all-to-all-start = ((bf16[8,32,768]{2,1,0:T(8,128)(2,1)}), bf16[8,32,768]{2,1,0:T(8,128)(2,1)}, u32[]{:S(2)}, u32[]{:S(2)}) async-start(bf16[8,32,768]{2,1,0:T(8,128)(2,1)} %bitcast.177), calls=%async_computation | async-start | bytes 786432 | tf_op jit(solution)/shard_map/all_to_all | solution.py:182
  157.6 173.4 %reduce-scatter.17.cloned.1.call-start = ((), (), s32[]{:S(2)}) async-start(), calls=%async_computation.10 | async-start | bytes 1327104 | tf_op jit(solution)/shard_map/reduce_scatter | solution.py:276
  180.2 15.4 %slice-start.13 = ((s8[4718592]{0:T(1024)(128)(4,1)}), s8[4194304]{0:T(1024)(128)(4,1)S(1)}, s32[]{:S(2)}) async-start(s8[4718592]{0:T(1024)(128)(4,1)} %bitcast.198), calls=%async_computation.31 | async-start | bytes 8388608
  225.0 21.5 %slice-start.6 = ((s8[12582912]{0:T(1024)(128)(4,1)}), s8[4194304]{0:T(1024)(128)(4,1)S(1)}, s32[]{:S(2)}) async-start(s8[12582912]{0:T(1024)(128)(4,1)} %bitcast.137), calls=%async_computation.24 | async-start | bytes 8388608
  225.0 21.5 %slice-start.7 = ((s8[12582912]{0:T(1024)(128)(4,1)}), s8[4194304]{0:T(1024)(128)(4,1)S(1)}, s32[]{:S(2)}) async-start(s8[12582912]{0:T(1024)(128)(4,1)} %bitcast.137), calls=%async_computation.25 | async-start | bytes 8388608
  256.1 145.7 %reduce-scatter.15.cloned.1.call-start = ((), (), s32[]{:S(2)}) async-start(), calls=%async_computation.9 | async-start | bytes 3981312 | tf_op jit(solution)/shard_map/reduce_scatter | solution.py:273
  303.3 197.0 %reduce-scatter.29.cloned.1.call-start = ((), (), s32[]{:S(2)}) async-start(), calls=%async_computation.16 | async-start | bytes 5308416
  320.7 278.1 %reduce-scatter.21.cloned.1.call-start = ((), (), s32[]{:S(2)}) async-start(), calls=%async_computation.12 | async-start | bytes 5308416 | tf_op jit(solution)/shard_map/reduce_scatter | solution.py:282
  330.9 290.4 %reduce-scatter.27.cloned.1.call-start = ((), (), s32[]{:S(2)}) async-start(), calls=%async_computation.15 | async-start | bytes 245760
  332.7 313.1 %reduce-scatter.25.cloned.1.call-start = ((), (), s32[]{:S(2)}) async-start(), calls=%async_computation.14 | async-start | bytes 737280
  403.9 266.6 %reduce-scatter.19.cloned.1.call-start = ((), (), s32[]{:S(2)}) async-start(), calls=%async_computation.11 | async-start | bytes 737280 | tf_op jit(solution)/shard_map/reduce_scatter | solution.py:293
  502.5 192.9 %reduce-scatter.23.cloned.1.call-start = ((), (), s32[]{:S(2)}) async-start(), calls=%async_computation.13 | async-start | bytes 737280 | tf_op jit(solution)/shard_map/reduce_scatter | solution.py:296
  598.8 139.8 %all-reduce.3.cloned.1.call-start = ((), (), s32[]{:S(2)}) async-start(), calls=%async_computation.17 | async-start | bytes 189440 | tf_op jit(solution)/shard_map/psum | solution.py:300
  (70 other events, 459.8 us)
Sparse Core Ops, SparseCore 0:
  256.3 63.7 reduce-scatter.16
  323.7 78.1 reduce-scatter.14
  405.5 94.8 reduce-scatter.28
  503.8 94.9 reduce-scatter.20
  601.7 19.5 reduce-scatter.26
  623.7 22.1 reduce-scatter.24
  648.5 22.0 reduce-scatter.18
  673.2 22.0 reduce-scatter.22
Sparse Core Ops, SparseCore 1:
  611.7 126.8 all-reduce.2
